TPU v7x, 32 devices: a whole 2x2x4 slice. The times are simulated.
32 devices in a mesh: grp: 2 (over y), tile: 4 (over z), span: 4 (over x, core).
Axes of the slice: x: 2, y: 2, z: 4, core: 2. Of those that a mesh axis runs over, the one named last changes fastest.
Arguments:
- features: bfloat16 [16, 8, 160, 384], P(('grp', 'span'), 'tile'), parts along dimension 0, may hold values from -24 to 24
- clip_lengths: int32 [8], P('grp'), parts along dimension 0, may hold values from 1 to 4, as said below
- norm_gain: float32 [384], replicated, may hold values from 0.1 to 1.9
- w_qkv: bfloat16 [384, 1152], replicated, may hold values from -6 to 6
- w_out: bfloat16 [384, 384], replicated, may hold values from -1 to 1
- conv_gain: float32 [384], replicated, may hold values from 0.1 to 1.9
- w_conv: bfloat16 [3, 3, 3, 384, 384], replicated, may hold values from -0.0625 to 0.0625
Outputs:
- attended: bfloat16 [16, 8, 160, 384], P(('grp', 'span'), 'tile'), parts along dimension 0
- hidden: bfloat16 [16, 8, 160, 384], P(('grp', 'span'), 'tile'), parts along dimension 0
There are 2 independent parts, one for each index of `grp`. A program takes and returns all parts, laid end to end along the dimension named above; an argument that names none is the same for every part. Nothing has to cross between parts.
Inputs may be any that keep to these rules, and one draw needn't show every extreme that they name: `clip_lengths`: the lengths sum to 8; exactly one clip has 4 frames.
All inputs are finite; a program needn't handle non-finite values.
Results may differ from a plain program's by a relative error of at most 0.0095.
The roundings to bfloat16 on the way count: a program that leaves them out, or rounds other values in their place, can miss the bound.
Values may be sent and summed in bfloat16 or wider, within the bound.
No kernel may reach another device: no remote copies, remote signals or barrier semaphores. Data moves between devices by JAX's collectives and lax.ppermute only.
A program may use at most 128 MiB of HBM per device.

v0:
```python
import jax
import jax.numpy as jnp
from jax import lax
from jax.sharding import PartitionSpec as P

eps = 1e-06


def from_behind(block, axis, distance):
    devices = range(lax.axis_size(axis))
    route = [(i - distance, i) for i in devices if i - distance in devices]
    return lax.ppermute(block, axis, route)


def extended(x, sides, width):
    for axis, dim in sides:
        size, length = (lax.axis_size(axis), x.shape[dim])
        up = [(i, (i + 1) % size) for i in range(size - 1)]
        down = [(j, i) for i, j in up]
        last = lax.slice_in_dim(x, length - width, length, axis=dim)
        first = lax.slice_in_dim(x, 0, width, axis=dim)
        before = lax.ppermute(last, axis, up)
        after = lax.ppermute(first, axis, down)
        x = jnp.concatenate([before, x, after], axis=dim)
    return x


def rms_scale(values, gain_vec):
    as_float = values.astype(jnp.float32)
    return (
        as_float * lax.rsqrt(jnp.mean(as_float * as_float, axis=-1, keepdims=True) + eps) * gain_vec
    )


def on_device(features, clip_lengths, norm_gain, w_qkv, w_out, conv_gain, w_conv):
    frames, row_count, col_count, channels = features.shape
    cell_count = row_count * col_count
    normed_grid = rms_scale(features, norm_gain).astype(jnp.bfloat16)
    view_frames = normed_grid.shape[0]
    view_cells = normed_grid.shape[1] * normed_grid.shape[2]
    normed = normed_grid.reshape(view_frames, view_cells, channels)
    queries = jnp.dot(
        normed.reshape(-1, channels), w_qkv[:, :channels], preferred_element_type=jnp.float32
    )
    queries = queries.astype(jnp.bfloat16).reshape(view_frames, view_cells, channels)
    kv_weight = w_qkv[:, channels:]
    score_scale = channels ** (-0.5)
    outgoing = jnp.dot(normed.reshape(-1, channels), kv_weight, preferred_element_type=jnp.float32)
    outgoing = outgoing.astype(jnp.bfloat16).reshape(view_frames, view_cells, 2 * channels)
    portion = lax.all_gather(outgoing, "tile", axis=1, tiled=True)
    key_part = portion[:, :, :channels]
    value_part = portion[:, :, channels:]
    row_top = jnp.full((view_frames, view_cells, 1), -1e30, jnp.float32)
    scores = (
        jnp.einsum("fqc,fkc->fqk", queries, key_part, preferred_element_type=jnp.float32)
        * score_scale
    )
    new_top = jnp.maximum(row_top, jnp.max(scores, axis=2, keepdims=True))
    raised_f = jnp.exp(scores - new_top)
    row_total = jnp.sum(raised_f, axis=2, keepdims=True)
    weighted = jnp.einsum(
        "fqk,fkc->fqc",
        raised_f.astype(jnp.bfloat16),
        value_part,
        preferred_element_type=jnp.float32,
    )
    mixture_grid = (weighted / row_total).astype(jnp.bfloat16)
    mixture = mixture_grid.reshape(-1, channels)
    projected = jnp.dot(mixture, w_out, preferred_element_type=jnp.float32)
    attended = (features.reshape(-1, channels).astype(jnp.float32) + projected).astype(jnp.bfloat16)
    attended = attended.reshape(frames, row_count, col_count, channels)
    lifted = rms_scale(attended, conv_gain)
    activated = (lifted * jax.nn.sigmoid(lifted)).astype(jnp.bfloat16)
    earlier = from_behind(activated, "span", 1)
    stacked = jnp.concatenate([earlier, activated], axis=0)
    edged = extended(stacked, (("tile", 1),), 1)
    padded = jnp.pad(edged, ((0, 0), (0, 0), (1, 1), (0, 0)))
    clip_ends = jnp.cumsum(clip_lengths)
    position = lax.axis_index("span") * frames + jnp.arange(frames, dtype=jnp.int32)
    clip_start = jnp.sum(
        jnp.where(clip_ends[None, :] <= position[:, None], clip_lengths[None, :], 0), axis=1
    )
    summed = jnp.zeros((frames * cell_count, channels), jnp.float32)
    for t_tap in range(3):
        usable = position - (2 - t_tap) >= clip_start
        for r_tap in range(3):
            for c_tap in range(3):
                shifted = padded[
                    t_tap : t_tap + frames, r_tap : r_tap + row_count, c_tap : c_tap + col_count
                ]
                shifted = jnp.where(
                    usable[:, None, None, None], shifted, jnp.zeros((), shifted.dtype)
                )
                summed = summed + jnp.dot(
                    shifted.reshape(-1, channels),
                    w_conv[t_tap, r_tap, c_tap],
                    preferred_element_type=jnp.float32,
                )
    hidden = summed.astype(jnp.bfloat16).reshape(frames, row_count, col_count, channels)
    return (attended, hidden)


def solution(mesh):
    in_specs = (P(("grp", "span"), "tile", None, None), P("grp"), P(), P(), P(), P(), P())
    out_specs = (P(("grp", "span"), "tile", None, None), P(("grp", "span"), "tile", None, None))
    return jax.shard_map(
        on_device, mesh=mesh, in_specs=in_specs, out_specs=out_specs, check_vma=False
    )
```

profile of v0, /device:TPU:10, one launch (start us, length us, event | category | flops | bytes accessed | tf_op | source)
XLA Modules:
  0.0 146.0 jit_solution(7980055820085720016)
XLA Ops:
  7.2 1.3 multiply_reduce_fusion
  8.5 1.2 multiply_convert_fusion.1
  9.8 2.7 %convolution_convert_fusion = bf16[640,768]{1,0:T(8,128)(2,1)} fusion(bf16[640,384]{1,0:T(8,128)(2,1)S(1)} %bitcast.177, bf16[384,1152]{1,0:T(8,128)(2,1)} %param.10), kind=kOutput, calls=%fused_computation.18 | convolution fusion | flops 377978880 | bytes 2064384 | tf_op jit(solution)/shard_map/dot_general | solution.py:48
  12.5 1.4 convolution_convert_fusion.1
  13.9 73.9 %all-gather.2.cloned.1.call-done = bf16[2,1280,768]{2,1,0:T(8,128)(2,1)} async-done(((bf16[2,320,768]{2,1,0:T(8,128)(2,1)}), bf16[2,1280,768]{2,1,0:T(8,128)(2,1)}) %all-gather.2.cloned.1.call-update) | async-done | bytes 3932176 | tf_op jit(solution)/shard_map/all_gather | solution.py:50
  87.8 2.8 %fusion.98 = (f32[2,320]{1,0:T(2,128)S(1)}, f32[2,320,1280]{2,1,0:T(8,128)S(1)}) fusion(bf16[2,320,384]{2,1,0:T(8,128)(2,1)S(1)} %bitcast.179, bf16[2,1280,768]{2,1,0:T(8,128)(2,1)} %all-gather.2.cloned.1.call-done), kind=kOutput, calls=%fused_computation.171 | convolution fusion | flops 630783360 | bytes 5736960 | tf_op jit(solution)/shard_map/fqc,fkc->fqk/dot_general | solution.py:55
  90.6 0.6 fusion.1
  91.3 1.1 divide_convert_fusion
  92.4 0.6 fusion.14
  93.5 1.9 %collective-permute-start = (bf16[2,2,160,384]{3,2,1,0:T(8,128)(2,1)S(1)}, bf16[2,2,160,384]{3,2,1,0:T(8,128)(2,1)S(1)}, u32[]{:S(2)}, u32[]{:S(2)}) collective-permute-start(bf16[2,2,160,384]{3,2,1,0:T(8,128)(2,1)S(1)} %multiply_convert_fusion), channel_id=1, source_target_pairs={{0,1},{1,2},{2,3},{4,5},{5,6},{6,7},{8,9},{9,10},{10,11},{12,13},{... | collective-permute-start | bytes 1474568 | tf_op jit(solution)/shard_map/ppermute | solution.py:12
  95.4 8.2 %collective-permute-done = bf16[2,2,160,384]{3,2,1,0:T(8,128)(2,1)S(1)} collective-permute-done((bf16[2,2,160,384]{3,2,1,0:T(8,128)(2,1)S(1)}, bf16[2,2,160,384]{3,2,1,0:T(8,128)(2,1)S(1)}, u32[]{:S(2)}, u32[]{:S(2)}) %collective-permute-start) | collective-permute-done | bytes 491552 | tf_op jit(solution)/shard_map/ppermute | solution.py:12
  103.6 0.9 fusion.30
  104.5 4.4 %collective-permute-start.1 = (bf16[4,1,160,384]{3,2,1,0:T(8,128)(2,1)}, bf16[4,1,160,384]{3,2,1,0:T(8,128)(2,1)S(1)}, u32[]{:S(2)}, u32[]{:S(2)}) collective-permute-start(bf16[4,1,160,384]{3,2,1,0:T(8,128)(2,1)} %get-tuple-element.34), channel_id=1, source_target_pairs={{0,4},{4,8},{8,12},{1,5},{5,9},{9,13},{2,6},{6,10},{10,14},{3,7},{... | collective-permute-start | bytes 1474568 | tf_op jit(solution)/shard_map/ppermute | solution.py:22
  108.9 1.9 %collective-permute-start.2 = (bf16[4,1,160,384]{3,2,1,0:T(8,128)(2,1)S(1)}, bf16[4,1,160,384]{3,2,1,0:T(8,128)(2,1)S(1)}, u32[]{:S(2)}, u32[]{:S(2)}) collective-permute-start(bf16[4,1,160,384]{3,2,1,0:T(8,128)(2,1)S(1)} %get-tuple-element.35), channel_id=1, source_target_pairs={{4,0},{8,4},{12,8},{5,1},{9,5},{13,9},{6,2},{10,6},{14,10},{7,3},{... | collective-permute-start | bytes 1474568 | tf_op jit(solution)/shard_map/ppermute | solution.py:23
  111.4 4.4 %collective-permute-done.1 = bf16[4,1,160,384]{3,2,1,0:T(8,128)(2,1)S(1)} collective-permute-done((bf16[4,1,160,384]{3,2,1,0:T(8,128)(2,1)}, bf16[4,1,160,384]{3,2,1,0:T(8,128)(2,1)S(1)}, u32[]{:S(2)}, u32[]{:S(2)}) %collective-permute-start.1) | collective-permute-done | bytes 491552 | tf_op jit(solution)/shard_map/ppermute | solution.py:22
  115.8 3.9 %collective-permute-done.2 = bf16[4,1,160,384]{3,2,1,0:T(8,128)(2,1)S(1)} collective-permute-done((bf16[4,1,160,384]{3,2,1,0:T(8,128)(2,1)S(1)}, bf16[4,1,160,384]{3,2,1,0:T(8,128)(2,1)S(1)}, u32[]{:S(2)}, u32[]{:S(2)}) %collective-permute-start.2) | collective-permute-done | bytes 491552 | tf_op jit(solution)/shard_map/ppermute | solution.py:23
  119.6 1.2 select_maximum_fusion
  120.8 1.4 slice_select_fusion
  122.5 1.5 %slice_select_fusion.6 = (bf16[2,2,160,384]{3,2,1,0:T(8,128)(2,1)S(1)}, bf16[2,2,160,384]{3,2,1,0:T(8,128)(2,1)S(1)}, bf16[2,2,160,384]{3,2,1,0:T(8,128)(2,1)S(1...) fusion(bf16[4,3,160,384]{3,2,1,0:T(8,128)(2,1)S(1)} %get-tuple-, ...), kind=kLoop, calls=%fused_computation.77 | loop fusion | flops 3686400 | bytes 13762566 | tf_op jit(solution)/shard_map/jit(_where)/select_n | solution.py:91
  124.3 1.3 slice-done.1
  126.5 0.5 convolution_add_fusion.24
  127.0 0.5 convolution_add_fusion.23
  127.5 0.5 convolution_add_fusion.22
  128.0 0.5 fusion.11
  128.4 0.5 convolution_add_fusion.20
  129.8 0.5 convolution_add_fusion.17
  130.3 0.5 convolution_add_fusion.16
  131.7 0.5 convolution_add_fusion.13
  132.1 0.5 convolution_add_fusion.12
  135.8 0.6 convolution_add_fusion.4
  136.5 0.5 convolution_add_fusion.3
  137.9 1.2 fusion.13
  (45 shorter events, 8.4 us)
Async XLA Ops:
  7.2 85.3 %copy-start = (bf16[384,384]{1,0:T(8,128)(2,1)S(1)}, bf16[384,384]{1,0:T(8,128)(2,1)}, u32[]{:S(2)}) copy-start(bf16[384,384]{1,0:T(8,128)(2,1)} %param.11) | copy-start | bytes 884740
  7.2 80.6 %all-gather.2.cloned.1.call-start = ((), (), s32[]{:S(2)}) async-start(), calls=%async_computation | async-start | bytes 4915200 | tf_op jit(solution)/shard_map/all_gather | solution.py:50
  87.8 3.5 %copy-start.2 = (bf16[2,1280,768]{2,1,0:T(8,128)(2,1)S(1)}, bf16[2,1280,768]{2,1,0:T(8,128)(2,1)}, u32[]{:S(2)}) copy-start(bf16[2,1280,768]{2,1,0:T(8,128)(2,1)} %all-gather.2.cloned.1.call-done) | copy-start | bytes 11796484
  91.3 1.1 copy-start.1
  91.3 1.8 %copy-start.4 = (f32[384]{0:T(512)S(1)}, f32[384]{0:T(512)}, u32[]{:S(2)}) copy-start(f32[384]{0:T(512)} %param.12) | copy-start | bytes 4612
  92.4 18.4 %copy-start.5 = (s32[4]{0:T(128)S(1)}, s32[4]{0:T(128)}, u32[]{:S(2)}) copy-start(s32[4]{0:T(128)} %param.8) | copy-start | bytes 52
  93.0 42.8 %copy-start.3 = (bf16[640,384]{1,0:T(8,128)(2,1)}, bf16[640,384]{1,0:T(8,128)(2,1)S(1)}, u32[]{:S(2)}) copy-start(bf16[640,384]{1,0:T(8,128)(2,1)S(1)} %get-tuple-element.55) | copy-start | bytes 1474564
  93.5 10.1 %collective-permute-start = (bf16[2,2,160,384]{3,2,1,0:T(8,128)(2,1)S(1)}, bf16[2,2,160,384]{3,2,1,0:T(8,128)(2,1)S(1)}, u32[]{:S(2)}, u32[]{:S(2)}) collective-permute-start(bf16[2,2,160,384]{3,2,1,0:T(8,128)(2,1)S(1)} %multiply_convert_fusion), channel_id=1, source_target_pairs={{0,1},{1,2},{2,3},{4,5},{5,6},{6,7},{8,9},{9,10},{10,11},{12,13},{... | collective-permute-start | bytes 1474568 | tf_op jit(solution)/shard_map/ppermute | solution.py:12
  104.5 11.2 %collective-permute-start.1 = (bf16[4,1,160,384]{3,2,1,0:T(8,128)(2,1)}, bf16[4,1,160,384]{3,2,1,0:T(8,128)(2,1)S(1)}, u32[]{:S(2)}, u32[]{:S(2)}) collective-permute-start(bf16[4,1,160,384]{3,2,1,0:T(8,128)(2,1)} %get-tuple-element.34), channel_id=1, source_target_pairs={{0,4},{4,8},{8,12},{1,5},{5,9},{9,13},{2,6},{6,10},{10,14},{3,7},{... | collective-permute-start | bytes 1474568 | tf_op jit(solution)/shard_map/ppermute | solution.py:22
  108.9 10.7 %collective-permute-start.2 = (bf16[4,1,160,384]{3,2,1,0:T(8,128)(2,1)S(1)}, bf16[4,1,160,384]{3,2,1,0:T(8,128)(2,1)S(1)}, u32[]{:S(2)}, u32[]{:S(2)}) collective-permute-start(bf16[4,1,160,384]{3,2,1,0:T(8,128)(2,1)S(1)} %get-tuple-element.35), channel_id=1, source_target_pairs={{4,0},{8,4},{12,8},{5,1},{9,5},{13,9},{6,2},{10,6},{14,10},{7,3},{... | collective-permute-start | bytes 1474568 | tf_op jit(solution)/shard_map/ppermute | solution.py:23
  122.2 2.1 %slice-start = ((s8[7962624]{0:T(1024)(128)(4,1)}), s8[3768320]{0:T(1024)(128)(4,1)S(1)}, s32[]{:S(2)}) async-start(s8[7962624]{0:T(1024)(128)(4,1)} %bitcast.148), calls=%async_computation.1 | async-start | bytes 7536640
  122.5 3.1 %slice-start.1 = ((s8[7962624]{0:T(1024)(128)(4,1)}), s8[4194304]{0:T(1024)(128)(4,1)S(1)}, s32[]{:S(2)}) async-start(s8[7962624]{0:T(1024)(128)(4,1)} %bitcast.148), calls=%async_computation.2 | async-start | bytes 8388608
Sparse Core Ops, SparseCore 0:
  12.6 75.1 all-gather.1
where the time goes:
time: 146 us
  waiting for transfers between devices  90.4 us (62%)
  matrix products  21.9 us (15%)
  between operations  14.4 us (10%)
  other arithmetic  9.18 us (6%)
  starting transfers between devices  8.25 us (6%)
  local copies, waits for them, and re-layouts  1.85 us (1%)
    all_gather x1, waiting for transfers between devices, on_device(): portion = lax.all_gather(outgoing, 'tile', axis=1, tiled=True)  73.9 us
    dot_general x27, matrix products, on_device(): jnp.dot(shifted.reshape(-1, channels), w_conv[t_tap, r_tap, c_tap], prefe...  13.3 us
    ppermute x1, waiting for transfers between devices, from_behind(): return lax.ppermute(block, axis, route)  8.22 us
    ppermute x1, starting transfers between devices, extended(): before = lax.ppermute(last, axis, up)  4.37 us
    ppermute x1, waiting for transfers between devices, extended(): before = lax.ppermute(last, axis, up)  4.36 us
    ppermute x1, waiting for transfers between devices, extended(): after = lax.ppermute(first, axis, down)  3.87 us
    select_n x2, other arithmetic, on_device(): jnp.where(usable[:, None, None, None], shifted, jnp.zeros((), shifted.dty...  2.92 us
  transfers between devices with their start and end apart: 4, of which 4 were waited for; matrix products, arithmetic and copies ran while one was open for 1% of the time, Pallas kernels for 0%

commit v1 on v0

--- a/solution.py
+++ b/solution.py
@@ -47,7 +47,21 @@
     score_scale = channels ** (-0.5)
     outgoing = jnp.dot(normed.reshape(-1, channels), kv_weight, preferred_element_type=jnp.float32)
     outgoing = outgoing.astype(jnp.bfloat16).reshape(view_frames, view_cells, 2 * channels)
-    portion = lax.all_gather(outgoing, "tile", axis=1, tiled=True)
+
+    def corner_post(mine, row_axis, axis_k):
+        parts_n = jax.lax.axis_size(row_axis)
+        gallery = [(p, (p + 1) % parts_n) for p in range(parts_n)]
+        work_now = [None] * parts_n
+        work_now[parts_n - 1] = mine
+        for dd in range(parts_n - 2, -1, -1):
+            work_now[dd] = jax.lax.ppermute(work_now[dd + 1], axis_name=row_axis, perm=gallery)
+        return jnp.roll(
+            jnp.concatenate(work_now, axis=axis_k),
+            (jax.lax.axis_index(row_axis) + 1) * mine.shape[axis_k],
+            axis=axis_k,
+        )
+
+    portion = corner_post(outgoing, "tile", 1)
     key_part = portion[:, :, :channels]
     value_part = portion[:, :, channels:]
     row_top = jnp.full((view_frames, view_cells, 1), -1e30, jnp.float32)

time: 146 us -> 130 us (0.89)
  between operations: 14.4 us -> 1.12 us
  waiting for transfers between devices: 90.4 us -> 81.2 us
  starting transfers between devices: 8.25 us -> 13.4 us
  local copies, waits for them, and re-layouts: 1.85 us -> 4.79 us
  matrix products: 21.9 us -> 20.1 us
    all_gather x1 -> x0, waiting for transfers between devices: 73.9 us -> none  [on_device(): portion = lax.all_gather(outgoing, 'tile', axis=1, tiled=True)]
    ppermute x0 -> x3, waiting for transfers between devices: none -> 64.7 us  [corner_post(): jax.lax.ppermute(work_now[dd + 1], axis_name=row_axis, perm=gallery)]
    ppermute x0 -> x3, starting transfers between devices: none -> 4.14 us  [corner_post(): jax.lax.ppermute(work_now[dd + 1], axis_name=row_axis, perm=gallery)]
    ppermute x1, starting transfers between devices: 1.92 us -> 5.44 us  [extended(): after = lax.ppermute(first, axis, down)]
    unnamed x16 -> x25, local copies, waits for them, and re-layouts: 1.61 us -> 4.48 us
    ppermute x1, starting transfers between devices: 4.37 us -> 1.92 us  [extended(): before = lax.ppermute(last, axis, up)]
    dot_general x1, matrix products: 2.83 us -> 1.18 us  [on_device(): jnp.einsum('fqc,fkc->fqk', queries, key_part, preferred_element_type=jnp....]
  transfers between devices with their start and end apart: 4 -> 6, of which waited for: 4 -> 6; matrix products, arithmetic and copies ran while one was open for 1% -> 2% of each run, Pallas kernels for 0% -> 0%
where the time goes in v1:
time: 130 us
  waiting for transfers between devices  81.2 us (62%)
  matrix products  20.1 us (15%)
  starting transfers between devices  13.4 us (10%)
  other arithmetic  9.18 us (7%)
  local copies, waits for them, and re-layouts  4.79 us (4%)
    ppermute x3, waiting for transfers between devices, corner_post(): jax.lax.ppermute(work_now[dd + 1], axis_name=row_axis, perm=gallery)  64.7 us
    dot_general x27, matrix products, on_device(): jnp.dot(shifted.reshape(-1, channels), w_conv[t_tap, r_tap, c_tap], prefe...  13.3 us
    ppermute x1, waiting for transfers between devices, from_behind(): return lax.ppermute(block, axis, route)  8.22 us
    ppermute x1, starting transfers between devices, extended(): after = lax.ppermute(first, axis, down)  5.44 us
    unnamed x25, local copies, waits for them, and re-layouts  4.48 us
    ppermute x1, waiting for transfers between devices, extended(): after = lax.ppermute(first, axis, down)  4.16 us
    ppermute x3, starting transfers between devices, corner_post(): jax.lax.ppermute(work_now[dd + 1], axis_name=row_axis, perm=gallery)  4.14 us
    ppermute x1, waiting for transfers between devices, extended(): before = lax.ppermute(last, axis, up)  4.08 us
  transfers between devices with their start and end apart: 6, of which 6 were waited for; matrix products, arithmetic and copies ran while one was open for 2% of the time, Pallas kernels for 0%

profile of v1, /device:TPU:10, one launch (start us, length us, event | category | flops | bytes accessed | tf_op | source)
XLA Modules:
  0.0 129.8 jit_solution(6268828413121387253)
XLA Ops:
  0.6 1.3 multiply_reduce_fusion
  2.0 1.2 multiply_convert_fusion.1
  3.2 1.9 %convolution_convert_fusion = bf16[640,768]{1,0:T(8,128)(2,1)S(1)} fusion(bf16[640,384]{1,0:T(8,128)(2,1)S(1)} %bitcast.170, bf16[384,1152]{1,0:T(8,128)(2,1)} %param.10), kind=kOutput, calls=%fused_computation.18 | convolution fusion | flops 377978880 | bytes 2064384 | tf_op jit(solution)/shard_map/dot_general | solution.py:48
  5.1 1.6 %collective-permute-start = (bf16[2,320,768]{2,1,0:T(8,128)(2,1)S(1)}, bf16[2,320,768]{2,1,0:T(8,128)(2,1)S(1)}, u32[]{:S(2)}, u32[]{:S(2)}) collective-permute-start(bf16[2,320,768]{2,1,0:T(8,128)(2,1)S(1)} %bitcast.150), channel_id=1, source_target_pairs={{0,4},{4,8},{8,12},{12,0},{1,5},{5,9},{9,13},{13,1},{2,6},{6,10},{... | collective-permute-start | bytes 2949128 | tf_op jit(solution)/shard_map/ppermute | solution.py:57
  6.7 21.9 %collective-permute-done = bf16[2,320,768]{2,1,0:T(8,128)(2,1)S(1)} collective-permute-done((bf16[2,320,768]{2,1,0:T(8,128)(2,1)S(1)}, bf16[2,320,768]{2,1,0:T(8,128)(2,1)S(1)}, u32[]{:S(2)}, u32[]{:S(2)}) %collective-permute-start) | collective-permute-done | bytes 983072 | tf_op jit(solution)/shard_map/ppermute | solution.py:57
  28.7 1.6 %collective-permute-start.1 = (bf16[2,320,768]{2,1,0:T(8,128)(2,1)S(1)}, bf16[2,320,768]{2,1,0:T(8,128)(2,1)S(1)}, u32[]{:S(2)}, u32[]{:S(2)}) collective-permute-start(bf16[2,320,768]{2,1,0:T(8,128)(2,1)S(1)} %collective-permute-done), channel_id=1, source_target_pairs={{0,4},{4,8},{8,12},{12,0},{1,5},{5,9},{9,13},{13,1},{2,6},{6,10},{... | collective-permute-start | bytes 2949128 | tf_op jit(solution)/shard_map/ppermute | solution.py:57
  30.2 21.7 %collective-permute-done.1 = bf16[2,320,768]{2,1,0:T(8,128)(2,1)S(1)} collective-permute-done((bf16[2,320,768]{2,1,0:T(8,128)(2,1)S(1)}, bf16[2,320,768]{2,1,0:T(8,128)(2,1)S(1)}, u32[]{:S(2)}, u32[]{:S(2)}) %collective-permute-start.1) | collective-permute-done | bytes 983072 | tf_op jit(solution)/shard_map/ppermute | solution.py:57
  51.9 0.9 collective-permute-start.2
  52.9 1.6 %convolution_convert_fusion.1 = bf16[640,384]{1,0:T(8,128)(2,1)S(1)} fusion(bf16[640,384]{1,0:T(8,128)(2,1)} %bitcast.171, bf16[384,1152]{1,0:T(8,128)(2,1)} %param.10), kind=kOutput, calls=%fused_computation.46 | convolution fusion | flops 188989440 | bytes 1277952 | tf_op jit(solution)/shard_map/dot_general | solution.py:42
  54.5 21.1 %collective-permute-done.2 = bf16[2,320,768]{2,1,0:T(8,128)(2,1)} collective-permute-done((bf16[2,320,768]{2,1,0:T(8,128)(2,1)S(1)}, bf16[2,320,768]{2,1,0:T(8,128)(2,1)}, u32[]{:S(2)}, u32[]{:S(2)}) %collective-permute-start.2) | collective-permute-done | bytes 983072 | tf_op jit(solution)/shard_map/ppermute | solution.py:57
  75.6 1.3 constant_dynamic-update-slice_fusion.7
  77.1 1.3 constant_dynamic-update-slice_fusion.3
  78.6 1.2 fusion.106
  79.8 0.6 fusion.1
  80.5 1.6 %fusion.19 = bf16[2,320,384]{2,1,0:T(8,128)(2,1)S(1)} fusion(bf16[2,2560,768]{2,1,0:T(8,128)(2,1)S(1)} %constant_dynamic-update-slice_fusion, s32[]{:T(128)S(6)} %select_n.101, s32[]{:T(128)S(6)} %add.186, f32[2,320,1280]{2,1,0:T(8,128)S(1)} %get-tuple-element.53, f32[2,320]{1,0:T(2,128)S(1)} %broadcast_maximum_fusion, f32[2,320]{1,0:T(2,128)S(1)} %fusion.1), kind=kOutput, calls=%fused_computation.56 | convolution fusion | flops 631275520 | bytes 5740552 | tf_op jit(solution)/shard_map/fqk,fkc->fqc/dot_general | solution.py:75
  82.0 0.6 fusion.24
  83.1 1.9 %collective-permute-start.3 = (bf16[2,2,160,384]{3,2,1,0:T(8,128)(2,1)S(1)}, bf16[2,2,160,384]{3,2,1,0:T(8,128)(2,1)S(1)}, u32[]{:S(2)}, u32[]{:S(2)}) collective-permute-start(bf16[2,2,160,384]{3,2,1,0:T(8,128)(2,1)S(1)} %multiply_convert_fusion), channel_id=1, source_target_pairs={{0,1},{1,2},{2,3},{4,5},{5,6},{6,7},{8,9},{9,10},{10,11},{12,13},{... | collective-permute-start | bytes 1474568 | tf_op jit(solution)/shard_map/ppermute | solution.py:12
  85.0 8.2 %collective-permute-done.3 = bf16[2,2,160,384]{3,2,1,0:T(8,128)(2,1)S(1)} collective-permute-done((bf16[2,2,160,384]{3,2,1,0:T(8,128)(2,1)S(1)}, bf16[2,2,160,384]{3,2,1,0:T(8,128)(2,1)S(1)}, u32[]{:S(2)}, u32[]{:S(2)}) %collective-permute-start.3) | collective-permute-done | bytes 491552 | tf_op jit(solution)/shard_map/ppermute | solution.py:12
  93.2 0.9 fusion.36
  94.1 5.4 %collective-permute-start.5 = (bf16[4,1,160,384]{3,2,1,0:T(8,128)(2,1)}, bf16[4,1,160,384]{3,2,1,0:T(8,128)(2,1)S(1)}, u32[]{:S(2)}, u32[]{:S(2)}) collective-permute-start(bf16[4,1,160,384]{3,2,1,0:T(8,128)(2,1)} %get-tuple-element.35), channel_id=1, source_target_pairs={{4,0},{8,4},{12,8},{5,1},{9,5},{13,9},{6,2},{10,6},{14,10},{7,3},{... | collective-permute-start | bytes 1474568 | tf_op jit(solution)/shard_map/ppermute | solution.py:23
  99.6 1.9 %collective-permute-start.4 = (bf16[4,1,160,384]{3,2,1,0:T(8,128)(2,1)S(1)}, bf16[4,1,160,384]{3,2,1,0:T(8,128)(2,1)S(1)}, u32[]{:S(2)}, u32[]{:S(2)}) collective-permute-start(bf16[4,1,160,384]{3,2,1,0:T(8,128)(2,1)S(1)} %get-tuple-element.34), channel_id=1, source_target_pairs={{0,4},{4,8},{8,12},{1,5},{5,9},{9,13},{2,6},{6,10},{10,14},{3,7},{... | collective-permute-start | bytes 1474568 | tf_op jit(solution)/shard_map/ppermute | solution.py:22
  102.1 4.2 %collective-permute-done.5 = bf16[4,1,160,384]{3,2,1,0:T(8,128)(2,1)S(1)} collective-permute-done((bf16[4,1,160,384]{3,2,1,0:T(8,128)(2,1)}, bf16[4,1,160,384]{3,2,1,0:T(8,128)(2,1)S(1)}, u32[]{:S(2)}, u32[]{:S(2)}) %collective-permute-start.5) | collective-permute-done | bytes 491552 | tf_op jit(solution)/shard_map/ppermute | solution.py:23
  106.2 4.1 %collective-permute-done.4 = bf16[4,1,160,384]{3,2,1,0:T(8,128)(2,1)S(1)} collective-permute-done((bf16[4,1,160,384]{3,2,1,0:T(8,128)(2,1)S(1)}, bf16[4,1,160,384]{3,2,1,0:T(8,128)(2,1)S(1)}, u32[]{:S(2)}, u32[]{:S(2)}) %collective-permute-start.4) | collective-permute-done | bytes 491552 | tf_op jit(solution)/shard_map/ppermute | solution.py:22
  110.3 1.2 select_maximum_fusion
  111.5 1.4 %slice_select_fusion = (bf16[2,2,160,384]{3,2,1,0:T(8,128)(2,1)S(1)}, bf16[2,2,160,384]{3,2,1,0:T(8,128)(2,1)S(1)}, bf16[2,2,160,384]{3,2,1,0:T(8,128)(2,1)S(1)}...) fusion(bf16[4,4,162,384]{3,2,1,0:T(8,128)(2,1)S(1)} %select_max, ...), kind=kLoop, calls=%fused_computation.72 | loop fusion | flops 2949120 | bytes 11796484 | tf_op jit(solution)/shard_map/jit(_where)/select_n | solution.py:105
  113.2 1.5 %slice_select_fusion.6 = (bf16[2,2,160,384]{3,2,1,0:T(8,128)(2,1)S(1)}, bf16[2,2,160,384]{3,2,1,0:T(8,128)(2,1)S(1)}, bf16[2,2,160,384]{3,2,1,0:T(8,128)(2,1)S(1...) fusion(bf16[4,3,160,384]{3,2,1,0:T(8,128)(2,1)S(1)} %get-tuple-, ...), kind=kLoop, calls=%fused_computation.78 | loop fusion | flops 3686400 | bytes 13762566 | tf_op jit(solution)/shard_map/jit(_where)/select_n | solution.py:105
  115.0 1.3 %slice-done.1 = s8[4194304]{0:T(1024)(128)(4,1)S(1)} async-done(((s8[7962624]{0:T(1024)(128)(4,1)}), s8[4194304]{0:T(1024)(128)(4,1)S(1)}, s32[]{:S(2)}) %slice-start.1) | async-done | bytes 4194328
  117.7 0.5 convolution_add_fusion.23
  119.1 0.5 convolution_add_fusion.20
  126.5 0.6 convolution_add_fusion.4
  127.2 0.5 convolution_add_fusion.3
  128.6 1.2 fusion.13
  (58 shorter events, 11.9 us)
Async XLA Ops:
  0.6 81.4 %copy-start = (bf16[384,384]{1,0:T(8,128)(2,1)S(1)}, bf16[384,384]{1,0:T(8,128)(2,1)}, u32[]{:S(2)}) copy-start(bf16[384,384]{1,0:T(8,128)(2,1)} %param.11) | copy-start | bytes 884740
  3.2 48.7 %copy-start.3 = (bf16[2,2,160,384]{3,2,1,0:T(8,128)(2,1)}, bf16[2,2,160,384]{3,2,1,0:T(8,128)(2,1)S(1)}, u32[]{:S(2)}) copy-start(bf16[2,2,160,384]{3,2,1,0:T(8,128)(2,1)S(1)} %multiply_convert_fusion.1) | copy-start | bytes 1474564
  5.1 23.5 %collective-permute-start = (bf16[2,320,768]{2,1,0:T(8,128)(2,1)S(1)}, bf16[2,320,768]{2,1,0:T(8,128)(2,1)S(1)}, u32[]{:S(2)}, u32[]{:S(2)}) collective-permute-start(bf16[2,320,768]{2,1,0:T(8,128)(2,1)S(1)} %bitcast.150), channel_id=1, source_target_pairs={{0,4},{4,8},{8,12},{12,0},{1,5},{5,9},{9,13},{13,1},{2,6},{6,10},{... | collective-permute-start | bytes 2949128 | tf_op jit(solution)/shard_map/ppermute | solution.py:57
  28.7 23.3 %collective-permute-start.1 = (bf16[2,320,768]{2,1,0:T(8,128)(2,1)S(1)}, bf16[2,320,768]{2,1,0:T(8,128)(2,1)S(1)}, u32[]{:S(2)}, u32[]{:S(2)}) collective-permute-start(bf16[2,320,768]{2,1,0:T(8,128)(2,1)S(1)} %collective-permute-done), channel_id=1, source_target_pairs={{0,4},{4,8},{8,12},{12,0},{1,5},{5,9},{9,13},{13,1},{2,6},{6,10},{... | collective-permute-start | bytes 2949128 | tf_op jit(solution)/shard_map/ppermute | solution.py:57
  51.9 23.7 %collective-permute-start.2 = (bf16[2,320,768]{2,1,0:T(8,128)(2,1)S(1)}, bf16[2,320,768]{2,1,0:T(8,128)(2,1)}, u32[]{:S(2)}, u32[]{:S(2)}) collective-permute-start(bf16[2,320,768]{2,1,0:T(8,128)(2,1)S(1)} %collective-permute-done.1), channel_id=1, source_target_pairs={{0,4},{4,8},{8,12},{12,0},{1,5},{5,9},{9,13},{13,1},{2,6},{6,10},{... | collective-permute-start | bytes 2949128 | tf_op jit(solution)/shard_map/ppermute | solution.py:57
  78.6 3.4 %copy-start.2 = (bf16[2,2,160,384]{3,2,1,0:T(8,128)(2,1)S(1)}, bf16[2,2,160,384]{3,2,1,0:T(8,128)(2,1)}, u32[]{:S(2)}) copy-start(bf16[2,2,160,384]{3,2,1,0:T(8,128)(2,1)} %param.7) | copy-start | bytes 1474564
  79.8 2.9 %copy-start.5 = (f32[384]{0:T(512)S(1)}, f32[384]{0:T(512)}, u32[]{:S(2)}) copy-start(f32[384]{0:T(512)} %param.12) | copy-start | bytes 4612
  79.8 21.7 %copy-start.6 = (s32[4]{0:T(128)S(1)}, s32[4]{0:T(128)}, u32[]{:S(2)}) copy-start(s32[4]{0:T(128)} %param.8) | copy-start | bytes 52
  82.6 43.9 %copy-start.4 = (bf16[640,384]{1,0:T(8,128)(2,1)}, bf16[640,384]{1,0:T(8,128)(2,1)S(1)}, u32[]{:S(2)}) copy-start(bf16[640,384]{1,0:T(8,128)(2,1)S(1)} %get-tuple-element.55) | copy-start | bytes 1474564
  83.1 10.1 %collective-permute-start.3 = (bf16[2,2,160,384]{3,2,1,0:T(8,128)(2,1)S(1)}, bf16[2,2,160,384]{3,2,1,0:T(8,128)(2,1)S(1)}, u32[]{:S(2)}, u32[]{:S(2)}) collective-permute-start(bf16[2,2,160,384]{3,2,1,0:T(8,128)(2,1)S(1)} %multiply_convert_fusion), channel_id=1, source_target_pairs={{0,1},{1,2},{2,3},{4,5},{5,6},{6,7},{8,9},{9,10},{10,11},{12,13},{... | collective-permute-start | bytes 1474568 | tf_op jit(solution)/shard_map/ppermute | solution.py:12
  94.1 12.1 %collective-permute-start.5 = (bf16[4,1,160,384]{3,2,1,0:T(8,128)(2,1)}, bf16[4,1,160,384]{3,2,1,0:T(8,128)(2,1)S(1)}, u32[]{:S(2)}, u32[]{:S(2)}) collective-permute-start(bf16[4,1,160,384]{3,2,1,0:T(8,128)(2,1)} %get-tuple-element.35), channel_id=1, source_target_pairs={{4,0},{8,4},{12,8},{5,1},{9,5},{13,9},{6,2},{10,6},{14,10},{7,3},{... | collective-permute-start | bytes 1474568 | tf_op jit(solution)/shard_map/ppermute | solution.py:23
  99.6 10.7 %collective-permute-start.4 = (bf16[4,1,160,384]{3,2,1,0:T(8,128)(2,1)S(1)}, bf16[4,1,160,384]{3,2,1,0:T(8,128)(2,1)S(1)}, u32[]{:S(2)}, u32[]{:S(2)}) collective-permute-start(bf16[4,1,160,384]{3,2,1,0:T(8,128)(2,1)S(1)} %get-tuple-element.34), channel_id=1, source_target_pairs={{0,4},{4,8},{8,12},{1,5},{5,9},{9,13},{2,6},{6,10},{10,14},{3,7},{... | collective-permute-start | bytes 1474568 | tf_op jit(solution)/shard_map/ppermute | solution.py:22
  112.9 2.1 %slice-start = ((s8[7962624]{0:T(1024)(128)(4,1)}), s8[3768320]{0:T(1024)(128)(4,1)S(1)}, s32[]{:S(2)}) async-start(s8[7962624]{0:T(1024)(128)(4,1)} %bitcast.148), calls=%async_computation | async-start | bytes 7536640
  113.2 3.1 %slice-start.1 = ((s8[7962624]{0:T(1024)(128)(4,1)}), s8[4194304]{0:T(1024)(128)(4,1)S(1)}, s32[]{:S(2)}) async-start(s8[7962624]{0:T(1024)(128)(4,1)} %bitcast.148), calls=%async_computation.1 | async-start | bytes 8388608
  126.0 3.8 %copy-start.1 = (bf16[384,384]{1,0:T(8,128)(2,1)S(1)}, bf16[384,384]{1,0:T(8,128)(2,1)}, u32[]{:S(2)}) copy-start(bf16[384,384]{1,0:T(8,128)(2,1)} %param.11) | copy-start | bytes 884740
